TPU v7x, 32 devices: a whole 2x2x4 slice. The times are simulated.
32 devices in a mesh: seq: 4 (over y, core), fsdp: 8 (over z, x).
Axes of the slice: x: 2, y: 2, z: 4, core: 2. Of those that a mesh axis runs over, the one named last changes fastest.
Arguments:
- latents: bfloat16 [8, 1536, 1536], P('fsdp', 'seq'), may hold values from -48 to 48
- qkv_weight: bfloat16 [1536, 768], P('fsdp'), may hold values from -1 to 1
- out_weight: bfloat16 [256, 1536], P('fsdp'), may hold values from -0.375 to 0.375
- tile_mask: int32 [4, 4], replicated, may hold values from 0 to 1, as said below
- tile_counts: int32 [4], replicated, may hold values from 64 to 384, as said below
Outputs:
- layer_out: bfloat16 [8, 1536, 1536], P('fsdp', 'seq')
Inputs may be any that keep to these rules, and one draw needn't show every extreme that they name: `tile_mask`: tiles are numbered frame first, then 2 along the height, then 2 along the width. Row q marks a box of whole tiles that contains tile q, of at most 4 tiles; row 0 marks exactly 4. `tile_counts`: the real tokens of a tile fill its first slots. Only tiles on the last frame index may be partial; a partial tile holds k * 64 tokens for some k of 1 to 6, the first tile of the last frame index is full, and the last tile is partial with k of 1 to 5.
All inputs are finite; a program needn't handle non-finite values.
Results may differ from a plain program's by a relative error of at most 0.0074.
Values may be sent and summed in bfloat16 or wider, within the bound.
No kernel may reach another device: no remote copies, remote signals or barrier semaphores. Data moves between devices by JAX's collectives and lax.ppermute only.
A program may use at most 64 MiB of HBM per device.

v0:
```python
import jax
import jax.numpy as jnp
from jax import lax
from jax.sharding import PartitionSpec as P

E = 64
TILE = 384
WINDOW = 4


def attend(queries, keys, values, tile_mask, tile_counts):
    tile_total = tile_mask.shape[0]
    score_scale = float(E) ** (-0.5)
    token_live = jnp.arange(TILE, dtype=jnp.int32)[None, :] < tile_counts[:, None]
    query_tiles = queries.reshape(tile_total, TILE, E)
    key_tiles_all = keys.reshape(tile_total, TILE, E)
    value_tiles_all = values.reshape(tile_total, TILE, E)
    tile_numbers = jnp.arange(tile_total, dtype=jnp.int32)

    def one_tile(tile_index):
        mask_row = tile_mask[tile_index]
        tile_order = jnp.argsort((1 - mask_row) * tile_total + tile_numbers)
        key_tiles = tile_order[:WINDOW]
        slot_live = jnp.arange(WINDOW, dtype=jnp.int32) < jnp.sum(mask_row)
        keys_sel = key_tiles_all[key_tiles].reshape(WINDOW * TILE, E)
        values_sel = value_tiles_all[key_tiles].reshape(WINDOW * TILE, E)
        allowed = (token_live[key_tiles] & slot_live[:, None]).reshape(WINDOW * TILE)[None, :]
        scores = (
            lax.dot_general(
                query_tiles[tile_index],
                keys_sel,
                (((1,), (1,)), ((), ())),
                preferred_element_type=jnp.float32,
            )
            * score_scale
        )
        masked = jnp.where(allowed, scores, -1e30)
        row_max = jnp.max(masked, axis=1, keepdims=True)
        numerators = jnp.where(allowed, jnp.exp(masked - row_max), 0.0)
        denominator = jnp.sum(numerators, axis=1, keepdims=True)
        softmax_top = numerators.astype(jnp.bfloat16)
        summed = jnp.dot(softmax_top, values_sel, preferred_element_type=jnp.float32) / denominator
        return jnp.where(token_live[tile_index][:, None], summed, 0.0).astype(jnp.bfloat16)

    return lax.map(one_tile, tile_numbers).reshape(tile_total * TILE, E)


def local(latents, qkv_weight, out_weight, tile_mask, tile_counts):
    seq_count = lax.axis_size("seq")
    local_rows = latents[0]
    row_count = local_rows.shape[0]
    column_count = qkv_weight.shape[1]
    head_columns = column_count // 3
    device_columns = head_columns // seq_count
    full_qkv = lax.all_gather(qkv_weight, "fsdp", axis=0, tiled=True)
    projected = jnp.dot(local_rows, full_qkv, preferred_element_type=jnp.float32)
    projected = projected.astype(jnp.bfloat16).reshape(row_count, 3, seq_count, device_columns)
    by_heads = lax.all_to_all(projected, "seq", split_axis=2, concat_axis=0, tiled=True)
    head_outputs = attend(
        by_heads[:, 0, 0, 0:E],
        by_heads[:, 1, 0, 0:E],
        by_heads[:, 2, 0, 0:E],
        tile_mask,
        tile_counts,
    )
    attended = head_outputs.reshape(seq_count, row_count, device_columns)
    by_tokens = lax.all_to_all(attended, "seq", split_axis=0, concat_axis=2, tiled=True)[0]
    full_out = lax.all_gather(out_weight, "fsdp", axis=0, tiled=True)
    layer_out = jnp.dot(by_tokens, full_out, preferred_element_type=jnp.float32)
    return layer_out.astype(jnp.bfloat16)[None]


def solution(mesh):
    return jax.shard_map(
        local,
        mesh=mesh,
        in_specs=(P("fsdp", "seq", None), P("fsdp", None), P("fsdp", None), P(), P()),
        out_specs=P("fsdp", "seq", None),
        check_vma=False,
    )
```

profile of v0, /device:TPU:0, one launch (start us, length us, event | category | flops | bytes accessed | tf_op | source)
XLA Modules:
  0.0 196.7 jit_solution(5970017230775210502)
XLA Ops:
  7.3 57.1 %all-gather.2.cloned.1.call-done = bf16[1536,768]{1,0:T(8,128)(2,1)} async-done(((bf16[192,768]{1,0:T(8,128)(2,1)}), bf16[1536,768]{1,0:T(8,128)(2,1)}) %all-gather.2.cloned.1.call-update) | async-done | bytes 2359312 | tf_op jit(solution)/shard_map/all_gather | solution.py:55
  64.4 2.7 %convolution_convert_fusion.1 = bf16[384,768]{1,0:T(8,128)(2,1)S(1)} fusion(bf16[1536,768]{1,0:T(8,128)(2,1)} %all-gather.2.cloned.1.call-done, bf16[1,384,1536]{2,1,0:T(8,128)(2,1)S(1)} %copy-done), kind=kOutput, calls=%fused_computation.31 | convolution fusion | flops 906264576 | bytes 4128768 | tf_op jit(solution)/shard_map/dot_general | solution.py:56
  68.3 3.5 %all-to-all-start = ((bf16[384,3,4,64]{0,3,1,2:T(8,128)(2,1)}), bf16[384,3,4,64]{0,3,1,2:T(8,128)(2,1)S(1)}, u32[]{:S(2)}, u32[]{:S(2)}) async-start(bf16[384,3,4,64]{0,3,1,2:T(8,128)(2,1)} %copy.12), calls=%async_computation | async-start | bytes 1179648 | tf_op jit(solution)/shard_map/all_to_all | solution.py:58
  71.9 9.4 %all-to-all-done = bf16[384,3,4,64]{0,3,1,2:T(8,128)(2,1)S(1)} async-done(((bf16[384,3,4,64]{0,3,1,2:T(8,128)(2,1)}), bf16[384,3,4,64]{0,3,1,2:T(8,128)(2,1)S(1)}, u32[]{:S(2)}, u32[]{:S(2)}) %all-to-all-start) | async-done | bytes 589856 | tf_op jit(solution)/shard_map/all_to_all | solution.py:58
  84.8 67.9 %while.11 = (s32[]{:T(128)}, bf16[4,384,64]{1,2,0:T(8,128)(2,1)}, s32[4]{0:T(128)}, pred[4,384]{1,0:T(4,128)(4,1)S(1)}, s32[4,4]{1,0:T(4,128)}, /*index=5*/bf16[...) while((s32[]{:T(128)}, bf16[4,384,64]{1,2,0:T(8,128)(2,1)}, ...), condition=%wide.region_5.6_spmd.clone, body=%wide.region_0.5_spmd.clone.sunk | while | flops 156378912 | bytes 8826411 | solution.py:45
  92.1 2.3 %gather_fusion.1 = bf16[4,384,64]{2,1,0:T(8,128)(2,1)} fusion(bf16[4,384,64]{2,1,0:T(8,128)(2,1)} %get-tuple-element.193, s32[1024]{0:T(1024)S(1)} %pad_clamp_fusion.2), kind=kCustom, calls=%fused_computation.1.clone.1 | custom fusion | bytes 393232 | tf_op jit(solution)/shard_map/while/body/eval_jaxpr/gather | solution.py:25
  94.4 1.6 fusion.48
  97.2 2.3 %gather_fusion = bf16[4,384,64]{2,1,0:T(8,128)(2,1)} fusion(bf16[4,384,64]{2,1,0:T(8,128)(2,1)} %get-tuple-element.194, s32[1024]{0:T(1024)S(1)} %pad_clamp_fusion.2), kind=kCustom, calls=%fused_computation.2.clone.1 | custom fusion | bytes 393232 | tf_op jit(solution)/shard_map/while/body/eval_jaxpr/gather | solution.py:26
  99.5 2.2 %fusion.50 = bf16[4,384,64]{1,2,0:T(8,128)(2,1)} fusion(bf16[4,384,64]{1,2,0:T(8,128)(2,1)} %get-tuple-element.177, s32[]{:T(128)} %get-tuple-element.176, bf16[1536,64]{1,0:T(8,128)(2,1)} %bitcast.56, f32[384,1536]{1,0:T(8,128)S(1)} %get-tuple-element.163, f32[384]{0:T(512)S(1)} %get-tuple-element.164, pred[1536]{0:T(1024)(128)(4,1)S(1)} %and.25, ...), kind=kOutput, calls=%fused_computation.16.clone.1 | convolution fusion | flops 77340672 | bytes 2807680 | tf_op jit(solution)/shard_map/while/body/eval_jaxpr/dot_general | solution.py:42
  109.1 2.3 %gather_fusion.1 = bf16[4,384,64]{2,1,0:T(8,128)(2,1)} fusion(bf16[4,384,64]{2,1,0:T(8,128)(2,1)} %get-tuple-element.193, s32[1024]{0:T(1024)S(1)} %pad_clamp_fusion.2), kind=kCustom, calls=%fused_computation.1.clone.1 | custom fusion | bytes 393232 | tf_op jit(solution)/shard_map/while/body/eval_jaxpr/gather | solution.py:25
  111.4 1.6 fusion.48
  114.1 2.3 %gather_fusion = bf16[4,384,64]{2,1,0:T(8,128)(2,1)} fusion(bf16[4,384,64]{2,1,0:T(8,128)(2,1)} %get-tuple-element.194, s32[1024]{0:T(1024)S(1)} %pad_clamp_fusion.2), kind=kCustom, calls=%fused_computation.2.clone.1 | custom fusion | bytes 393232 | tf_op jit(solution)/shard_map/while/body/eval_jaxpr/gather | solution.py:26
  116.5 2.2 %fusion.50 = bf16[4,384,64]{1,2,0:T(8,128)(2,1)} fusion(bf16[4,384,64]{1,2,0:T(8,128)(2,1)} %get-tuple-element.177, s32[]{:T(128)} %get-tuple-element.176, bf16[1536,64]{1,0:T(8,128)(2,1)} %bitcast.56, f32[384,1536]{1,0:T(8,128)S(1)} %get-tuple-element.163, f32[384]{0:T(512)S(1)} %get-tuple-element.164, pred[1536]{0:T(1024)(128)(4,1)S(1)} %and.25, ...), kind=kOutput, calls=%fused_computation.16.clone.1 | convolution fusion | flops 77340672 | bytes 2807680 | tf_op jit(solution)/shard_map/while/body/eval_jaxpr/dot_general | solution.py:42
  126.1 2.3 %gather_fusion.1 = bf16[4,384,64]{2,1,0:T(8,128)(2,1)} fusion(bf16[4,384,64]{2,1,0:T(8,128)(2,1)} %get-tuple-element.193, s32[1024]{0:T(1024)S(1)} %pad_clamp_fusion.2), kind=kCustom, calls=%fused_computation.1.clone.1 | custom fusion | bytes 393232 | tf_op jit(solution)/shard_map/while/body/eval_jaxpr/gather | solution.py:25
  128.4 1.6 fusion.48
  131.1 2.3 %gather_fusion = bf16[4,384,64]{2,1,0:T(8,128)(2,1)} fusion(bf16[4,384,64]{2,1,0:T(8,128)(2,1)} %get-tuple-element.194, s32[1024]{0:T(1024)S(1)} %pad_clamp_fusion.2), kind=kCustom, calls=%fused_computation.2.clone.1 | custom fusion | bytes 393232 | tf_op jit(solution)/shard_map/while/body/eval_jaxpr/gather | solution.py:26
  133.5 2.2 %fusion.50 = bf16[4,384,64]{1,2,0:T(8,128)(2,1)} fusion(bf16[4,384,64]{1,2,0:T(8,128)(2,1)} %get-tuple-element.177, s32[]{:T(128)} %get-tuple-element.176, bf16[1536,64]{1,0:T(8,128)(2,1)} %bitcast.56, f32[384,1536]{1,0:T(8,128)S(1)} %get-tuple-element.163, f32[384]{0:T(512)S(1)} %get-tuple-element.164, pred[1536]{0:T(1024)(128)(4,1)S(1)} %and.25, ...), kind=kOutput, calls=%fused_computation.16.clone.1 | convolution fusion | flops 77340672 | bytes 2807680 | tf_op jit(solution)/shard_map/while/body/eval_jaxpr/dot_general | solution.py:42
  143.0 2.3 %gather_fusion.1 = bf16[4,384,64]{2,1,0:T(8,128)(2,1)} fusion(bf16[4,384,64]{2,1,0:T(8,128)(2,1)} %get-tuple-element.193, s32[1024]{0:T(1024)S(1)} %pad_clamp_fusion.2), kind=kCustom, calls=%fused_computation.1.clone.1 | custom fusion | bytes 393232 | tf_op jit(solution)/shard_map/while/body/eval_jaxpr/gather | solution.py:25
  145.4 1.6 fusion.48
  148.1 2.3 %gather_fusion = bf16[4,384,64]{2,1,0:T(8,128)(2,1)} fusion(bf16[4,384,64]{2,1,0:T(8,128)(2,1)} %get-tuple-element.194, s32[1024]{0:T(1024)S(1)} %pad_clamp_fusion.2), kind=kCustom, calls=%fused_computation.2.clone.1 | custom fusion | bytes 393232 | tf_op jit(solution)/shard_map/while/body/eval_jaxpr/gather | solution.py:26
  150.5 2.2 %fusion.50 = bf16[4,384,64]{1,2,0:T(8,128)(2,1)} fusion(bf16[4,384,64]{1,2,0:T(8,128)(2,1)} %get-tuple-element.177, s32[]{:T(128)} %get-tuple-element.176, bf16[1536,64]{1,0:T(8,128)(2,1)} %bitcast.56, f32[384,1536]{1,0:T(8,128)S(1)} %get-tuple-element.163, f32[384]{0:T(512)S(1)} %get-tuple-element.164, pred[1536]{0:T(1024)(128)(4,1)S(1)} %and.25, ...), kind=kOutput, calls=%fused_computation.16.clone.1 | convolution fusion | flops 77340672 | bytes 2807680 | tf_op jit(solution)/shard_map/while/body/eval_jaxpr/dot_general | solution.py:42
  152.7 3.4 %all-to-all-start.1 = ((bf16[4,384,64]{1,2,0:T(8,128)(2,1)}), bf16[4,384,64]{1,2,0:T(8,128)(2,1)S(1)}, u32[]{:S(2)}, u32[]{:S(2)}) async-start(bf16[4,384,64]{1,2,0:T(8,128)(2,1)} %get-tuple-element.51), calls=%async_computation.1 | async-start | bytes 393216 | tf_op jit(solution)/shard_map/all_to_all | solution.py:67
  156.1 32.3 %all_gather.7 = bf16[256,1536]{1,0:T(8,128)(2,1)S(1)} all-gather(bf16[32,1536]{1,0:T(8,128)(2,1)} %param.9), channel_id=1, replica_groups=mesh['seq'=4,'fsdp'=8] {'fsdp'}, dimensions={0}, use_global_device_ids=true | all-gather | bytes 884736 | tf_op jit(solution)/shard_map/all_gather | solution.py:68
  188.3 1.5 fusion.28
  (69 shorter events, 31.6 us)
Async XLA Ops:
  6.5 57.8 %copy-start = (bf16[1,384,1536]{2,1,0:T(8,128)(2,1)S(1)}, bf16[1,384,1536]{2,1,0:T(8,128)(2,1)}, u32[]{:S(2)}) copy-start(bf16[1,384,1536]{2,1,0:T(8,128)(2,1)} %param.7) | copy-start | bytes 3538948
  6.5 57.8 %all-gather.2.cloned.1.call-start = ((), (), s32[]{:S(2)}) async-start(), calls=%async_computation.2 | async-start | bytes 2654208 | tf_op jit(solution)/shard_map/all_gather | solution.py:55
  67.1 4.7 %copy-start.1 = (s32[4]{0:T(128)S(1)}, s32[4]{0:T(128)}, u32[]{:S(2)}) copy-start(s32[4]{0:T(128)} %param.11) | copy-start | bytes 52
  68.3 13.0 %all-to-all-start = ((bf16[384,3,4,64]{0,3,1,2:T(8,128)(2,1)}), bf16[384,3,4,64]{0,3,1,2:T(8,128)(2,1)S(1)}, u32[]{:S(2)}, u32[]{:S(2)}) async-start(bf16[384,3,4,64]{0,3,1,2:T(8,128)(2,1)} %copy.12), calls=%async_computation | async-start | bytes 1179648 | tf_op jit(solution)/shard_map/all_to_all | solution.py:58
  152.7 35.6 %all-to-all-start.1 = ((bf16[4,384,64]{1,2,0:T(8,128)(2,1)}), bf16[4,384,64]{1,2,0:T(8,128)(2,1)S(1)}, u32[]{:S(2)}, u32[]{:S(2)}) async-start(bf16[4,384,64]{1,2,0:T(8,128)(2,1)} %get-tuple-element.51), calls=%async_computation.1 | async-start | bytes 393216 | tf_op jit(solution)/shard_map/all_to_all | solution.py:67
Sparse Core Ops, SparseCore 0:
  9.5 54.7 all-gather.1
where the time goes:
time: 198 us; the launch traced here: 197 us
  waiting for transfers between devices  67.2 us (34%)
  blocking collectives  32.3 us (16%)
  local copies, waits for them, and re-layouts  30.9 us (16%)
  matrix products  19.6 us (10%)
  other arithmetic  18.7 us (9%)
  between operations  13.5 us (7%)
  loops' own time  7.68 us (4%)
  starting transfers between devices  6.84 us (3%)
    all_gather x1, waiting for transfers between devices, local(): full_qkv = lax.all_gather(qkv_weight, 'fsdp', axis=0, tiled=True)  57.1 us
    all_gather x1, blocking collectives, local(): full_out = lax.all_gather(out_weight, 'fsdp', axis=0, tiled=True)  32.3 us
    all_to_all x1, waiting for transfers between devices, local(): lax.all_to_all(projected, 'seq', split_axis=2, concat_axis=0, tiled=True)  9.42 us
    gather x4, local copies, waits for them, and re-layouts, one_tile(): keys_sel = key_tiles_all[key_tiles].reshape(WINDOW * TILE, E)  9.34 us
    gather x4, local copies, waits for them, and re-layouts, one_tile(): values_sel = value_tiles_all[key_tiles].reshape(WINDOW * TILE, E)  9.34 us
    dot_general x4, matrix products, one_tile(): jnp.dot(softmax_top, values_sel, preferred_element_type=jnp.float32)  8.88 us
    another operation x1, loops' own time, attend(): return lax.map(one_tile, tile_numbers).reshape(tile_total * TILE, E)  7.68 us
    dot_general x4, matrix products, one_tile(): lax.dot_general(query_tiles[tile_index], keys_sel, (((1,), (1,)), ((), ()...  6.5 us
  transfers between devices with their start and end apart: 3, of which 2 were waited for; matrix products, arithmetic and copies ran while one was open for 0% of the time, Pallas kernels for 0%

commit v1 on v0

--- a/solution.py
+++ b/solution.py
@@ -65,7 +65,21 @@
     )
     attended = head_outputs.reshape(seq_count, row_count, device_columns)
     by_tokens = lax.all_to_all(attended, "seq", split_axis=0, concat_axis=2, tiled=True)[0]
-    full_out = lax.all_gather(out_weight, "fsdp", axis=0, tiled=True)
+    new = lax.axis_size("fsdp")
+    upper, step_out, even = (new, lax.axis_index("fsdp"), out_weight.shape[0])
+    lower, clean = (out_weight, 1)
+    while clean < upper:
+        lower = jnp.concatenate(
+            [
+                lower,
+                lax.ppermute(
+                    lower, "fsdp", [(hop_no, (hop_no - clean) % upper) for hop_no in range(upper)]
+                ),
+            ],
+            axis=0,
+        )
+        clean = 2 * clean
+    full_out = jnp.roll(lower, step_out * even, axis=0)
     layer_out = jnp.dot(by_tokens, full_out, preferred_element_type=jnp.float32)
     return layer_out.astype(jnp.bfloat16)[None]
 

time: 198 us -> 159 us (0.80)
  blocking collectives: 32.3 us -> 0 us
  local copies, waits for them, and re-layouts: 30.9 us -> 19.5 us
  starting transfers between devices: 6.84 us -> 14.6 us
  matrix products: 19.6 us -> 12.5 us
  waiting for transfers between devices: 67.2 us -> 70.3 us
    all_gather x1 -> x0, blocking collectives: 32.3 us -> none  [local(): full_out = lax.all_gather(out_weight, 'fsdp', axis=0, tiled=True)]
    all_gather x1, waiting for transfers between devices: 57.1 us -> 24.9 us  [local(): full_qkv = lax.all_gather(qkv_weight, 'fsdp', axis=0, tiled=True)]
    ppermute x0 -> x3, waiting for transfers between devices: none -> 31.9 us  [local(): lax.ppermute(lower, 'fsdp', [(hop_no, (hop_no - clean) % upper) for hop_n...]
    ppermute x0 -> x3, starting transfers between devices: none -> 7.76 us  [local(): lax.ppermute(lower, 'fsdp', [(hop_no, (hop_no - clean) % upper) for hop_n...]
    gather x4, local copies, waits for them, and re-layouts: 9.34 us -> 2.49 us  [one_tile(): values_sel = value_tiles_all[key_tiles].reshape(WINDOW * TILE, E)]
    gather x4, local copies, waits for them, and re-layouts: 9.34 us -> 2.49 us  [one_tile(): keys_sel = key_tiles_all[key_tiles].reshape(WINDOW * TILE, E)]
    all_to_all x1, waiting for transfers between devices: 0.01 us -> 4.53 us  [local(): lax.all_to_all(attended, 'seq', split_axis=0, concat_axis=2, tiled=True)[0]]
    dot_general x4, matrix products: 6.5 us -> 2.28 us  [one_tile(): lax.dot_general(query_tiles[tile_index], keys_sel, (((1,), (1,)), ((), ()...]
  transfers between devices with their start and end apart: 3 -> 6, of which waited for: 2 -> 6; matrix products, arithmetic and copies ran while one was open for 0% -> 4% of each run, Pallas kernels for 0% -> 0%
where the time goes in v1:
time: 159 us; the launch traced here: 158 us
  waiting for transfers between devices  70.3 us (44%)
  other arithmetic  19.6 us (12%)
  local copies, waits for them, and re-layouts  19.5 us (12%)
  starting transfers between devices  14.6 us (9%)
  between operations  13.5 us (8%)
  matrix products  12.5 us (8%)
  loops' own time  8.42 us (5%)
    ppermute x3, waiting for transfers between devices, local(): lax.ppermute(lower, 'fsdp', [(hop_no, (hop_no - clean) % upper) for hop_n...  31.9 us
    all_gather x1, waiting for transfers between devices, local(): full_qkv = lax.all_gather(qkv_weight, 'fsdp', axis=0, tiled=True)  24.9 us
    another operation x1, loops' own time, attend(): return lax.map(one_tile, tile_numbers).reshape(tile_total * TILE, E)  8.42 us
    all_to_all x1, waiting for transfers between devices, local(): lax.all_to_all(projected, 'seq', split_axis=2, concat_axis=0, tiled=True)  8.18 us
    ppermute x3, starting transfers between devices, local(): lax.ppermute(lower, 'fsdp', [(hop_no, (hop_no - clean) % upper) for hop_n...  7.76 us
    reduce_sum x4, other arithmetic, one_tile(): slot_live = jnp.arange(WINDOW, dtype=jnp.int32) < jnp.sum(mask_row)  5.61 us
    dynamic_slice x4, local copies, waits for them, and re-layouts, attend(): return lax.map(one_tile, tile_numbers).reshape(tile_total * TILE, E)  5.27 us
    dot_general x4, matrix products, one_tile(): jnp.dot(softmax_top, values_sel, preferred_element_type=jnp.float32)  4.85 us
  transfers between devices with their start and end apart: 6, of which 6 were waited for; matrix products, arithmetic and copies ran while one was open for 4% of the time, Pallas kernels for 0%

profile of v1, /device:TPU:0, one launch (start us, length us, event | category | flops | bytes accessed | tf_op | source)
XLA Modules:
  0.0 158.3 jit_solution(17350358727004289466)
XLA Ops:
  7.3 6.0 %collective-permute-start = (bf16[32,1536]{1,0:T(8,128)(2,1)}, bf16[32,1536]{1,0:T(8,128)(2,1)S(1)}, u32[]{:S(2)}, u32[]{:S(2)}) collective-permute-start(bf16[32,1536]{1,0:T(8,128)(2,1)} %param.9), channel_id=1, source_target_pairs={{0,7},{1,0},{2,1},{3,2},{4,3},{5,4},{6,5},{7,6},{8,15},{9,8},{10,9... | collective-permute-start | bytes 294920 | tf_op jit(solution)/shard_map/ppermute | solution.py:75
  14.2 1.6 %collective-permute-done = bf16[32,1536]{1,0:T(8,128)(2,1)S(1)} collective-permute-done((bf16[32,1536]{1,0:T(8,128)(2,1)}, bf16[32,1536]{1,0:T(8,128)(2,1)S(1)}, u32[]{:S(2)}, u32[]{:S(2)}) %collective-permute-start) | collective-permute-done | bytes 98336 | tf_op jit(solution)/shard_map/ppermute | solution.py:75
  16.7 1.4 collective-permute-start.1
  18.9 3.7 %collective-permute-done.1 = bf16[64,1536]{1,0:T(8,128)(2,1)S(1)} collective-permute-done((bf16[64,1536]{1,0:T(8,128)(2,1)S(1)}, bf16[64,1536]{1,0:T(8,128)(2,1)S(1)}, u32[]{:S(2)}, u32[]{:S(2)}) %collective-permute-start.1) | collective-permute-done | bytes 196640 | tf_op jit(solution)/shard_map/ppermute | solution.py:75
  23.8 26.6 %collective-permute-done.2 = bf16[128,1536]{1,0:T(8,128)(2,1)S(1)} collective-permute-done((bf16[128,1536]{1,0:T(8,128)(2,1)S(1)}, bf16[128,1536]{1,0:T(8,128)(2,1)S(1)}, u32[]{:S(2)}, u32[]{:S(2)}) %collective-permute-start.2) | collective-permute-done | bytes 393248 | tf_op jit(solution)/shard_map/ppermute | solution.py:75
  51.7 24.9 %all-gather.2.cloned.1.call-done = bf16[1536,768]{1,0:T(8,128)(2,1)} async-done(((bf16[192,768]{1,0:T(8,128)(2,1)}), bf16[1536,768]{1,0:T(8,128)(2,1)}) %all-gather.2.cloned.1.call-update) | async-done | bytes 2359312 | tf_op jit(solution)/shard_map/all_gather | solution.py:55
  76.6 2.7 %convolution_convert_fusion.1 = bf16[384,768]{1,0:T(8,128)(2,1)S(1)} fusion(bf16[1536,768]{1,0:T(8,128)(2,1)} %all-gather.2.cloned.1.call-done, bf16[1,384,1536]{2,1,0:T(8,128)(2,1)S(1)} %copy-done), kind=kOutput, calls=%fused_computation.31 | convolution fusion | flops 906264576 | bytes 4128768 | tf_op jit(solution)/shard_map/dot_general | solution.py:56
  80.5 3.5 %all-to-all-start = ((bf16[384,3,4,64]{0,3,1,2:T(8,128)(2,1)}), bf16[384,3,4,64]{0,3,1,2:T(8,128)(2,1)S(1)}, u32[]{:S(2)}, u32[]{:S(2)}) async-start(bf16[384,3,4,64]{0,3,1,2:T(8,128)(2,1)} %copy.12), calls=%async_computation | async-start | bytes 1179648 | tf_op jit(solution)/shard_map/all_to_all | solution.py:58
  85.3 8.2 %all-to-all-done = bf16[384,3,4,64]{0,3,1,2:T(8,128)(2,1)S(1)} async-done(((bf16[384,3,4,64]{0,3,1,2:T(8,128)(2,1)}), bf16[384,3,4,64]{0,3,1,2:T(8,128)(2,1)S(1)}, u32[]{:S(2)}, u32[]{:S(2)}) %all-to-all-start) | async-done | bytes 589856 | tf_op jit(solution)/shard_map/all_to_all | solution.py:58
  94.9 45.3 %while.11 = (s32[]{:T(128)}, bf16[4,384,64]{1,2,0:T(8,128)(2,1)}, s32[4]{0:T(128)}, pred[4,384]{1,0:T(4,128)(4,1)S(1)}, s32[4,4]{1,0:T(4,128)}, /*index=5*/bf16[...) while((s32[]{:T(128)}, bf16[4,384,64]{1,2,0:T(8,128)(2,1)}, ...), condition=%wide.region_5.6_spmd.clone, body=%wide.region_0.5_spmd.clone.sunk | while | flops 156378912 | bytes 8629303 | solution.py:45
  94.9 1.3 dynamic_slice.45
  101.6 1.4 fusion.48
  105.0 1.2 fusion.51
  106.2 1.3 dynamic_slice.45
  113.0 1.4 fusion.48
  117.5 1.3 dynamic_slice.45
  124.3 1.4 fusion.48
  127.6 1.2 fusion.51
  128.8 1.3 dynamic_slice.45
  135.6 1.4 fusion.48
  138.9 1.2 fusion.51
  140.1 3.4 %all-to-all-start.1 = ((bf16[4,384,64]{1,2,0:T(8,128)(2,1)}), bf16[4,384,64]{1,2,0:T(8,128)(2,1)S(1)}, u32[]{:S(2)}, u32[]{:S(2)}) async-start(bf16[4,384,64]{1,2,0:T(8,128)(2,1)} %get-tuple-element.51), calls=%async_computation.1 | async-start | bytes 393216 | tf_op jit(solution)/shard_map/all_to_all | solution.py:67
  144.3 4.5 %all-to-all-done.1 = bf16[4,384,64]{1,2,0:T(8,128)(2,1)S(1)} async-done(((bf16[4,384,64]{1,2,0:T(8,128)(2,1)}), bf16[4,384,64]{1,2,0:T(8,128)(2,1)S(1)}, u32[]{:S(2)}, u32[]{:S(2)}) %all-to-all-start.1) | async-done | bytes 196640 | tf_op jit(solution)/shard_map/all_to_all | solution.py:67
  148.8 2.6 %fusion.28 = bf16[1,384,1536]{2,1,0:T(8,128)(2,1)} fusion(bf16[384,256]{0,1:T(8,128)(2,1)S(1)} %bitcast.61, bf16[512,1536]{1,0:T(8,128)(2,1)} %constant_dynamic-update-slice_fusion, s32[]{:T(128)S(6)} %select_n.35), kind=kOutput, calls=%fused_computation.30 | convolution fusion | flops 302579712 | bytes 2162692 | tf_op jit(solution)/shard_map/dot_general | solution.py:83
  (86 shorter events, 32.6 us)
Async XLA Ops:
  6.5 70.1 %copy-start = (bf16[1,384,1536]{2,1,0:T(8,128)(2,1)S(1)}, bf16[1,384,1536]{2,1,0:T(8,128)(2,1)}, u32[]{:S(2)}) copy-start(bf16[1,384,1536]{2,1,0:T(8,128)(2,1)} %param.7) | copy-start | bytes 3538948
  6.5 44.0 %copy-start.1 = (bf16[32,1536]{1,0:T(8,128)(2,1)S(1)}, bf16[32,1536]{1,0:T(8,128)(2,1)}, u32[]{:S(2)}) copy-start(bf16[32,1536]{1,0:T(8,128)(2,1)} %param.9) | copy-start | bytes 294916
  6.5 70.0 %all-gather.2.cloned.1.call-start = ((), (), s32[]{:S(2)}) async-start(), calls=%async_computation.2 | async-start | bytes 2654208 | tf_op jit(solution)/shard_map/all_gather | solution.py:55
  7.3 8.6 %collective-permute-start = (bf16[32,1536]{1,0:T(8,128)(2,1)}, bf16[32,1536]{1,0:T(8,128)(2,1)S(1)}, u32[]{:S(2)}, u32[]{:S(2)}) collective-permute-start(bf16[32,1536]{1,0:T(8,128)(2,1)} %param.9), channel_id=1, source_target_pairs={{0,7},{1,0},{2,1},{3,2},{4,3},{5,4},{6,5},{7,6},{8,15},{9,8},{10,9... | collective-permute-start | bytes 294920 | tf_op jit(solution)/shard_map/ppermute | solution.py:75
  16.7 5.8 %collective-permute-start.1 = (bf16[64,1536]{1,0:T(8,128)(2,1)S(1)}, bf16[64,1536]{1,0:T(8,128)(2,1)S(1)}, u32[]{:S(2)}, u32[]{:S(2)}) collective-permute-start(bf16[64,1536]{1,0:T(8,128)(2,1)S(1)} %pad_maximum_fusion.1), channel_id=1, source_target_pairs={{0,6},{1,7},{2,0},{3,1},{4,2},{5,3},{6,4},{7,5},{8,14},{9,15},{10,... | collective-permute-start | bytes 589832 | tf_op jit(solution)/shard_map/ppermute | solution.py:75
  23.5 27.0 %collective-permute-start.2 = (bf16[128,1536]{1,0:T(8,128)(2,1)S(1)}, bf16[128,1536]{1,0:T(8,128)(2,1)S(1)}, u32[]{:S(2)}, u32[]{:S(2)}) collective-permute-start(bf16[128,1536]{1,0:T(8,128)(2,1)S(1)} %pad_maximum_fusion), channel_id=1, source_target_pairs={{0,4},{1,5},{2,6},{3,7},{4,0},{5,1},{6,2},{7,3},{8,12},{9,13},{10,... | collective-permute-start | bytes 1179656 | tf_op jit(solution)/shard_map/ppermute | solution.py:75
  50.5 1.2 copy-start.2
  80.5 13.0 %all-to-all-start = ((bf16[384,3,4,64]{0,3,1,2:T(8,128)(2,1)}), bf16[384,3,4,64]{0,3,1,2:T(8,128)(2,1)S(1)}, u32[]{:S(2)}, u32[]{:S(2)}) async-start(bf16[384,3,4,64]{0,3,1,2:T(8,128)(2,1)} %copy.12), calls=%async_computation | async-start | bytes 1179648 | tf_op jit(solution)/shard_map/all_to_all | solution.py:58
  140.1 8.7 %all-to-all-start.1 = ((bf16[4,384,64]{1,2,0:T(8,128)(2,1)}), bf16[4,384,64]{1,2,0:T(8,128)(2,1)S(1)}, u32[]{:S(2)}, u32[]{:S(2)}) async-start(bf16[4,384,64]{1,2,0:T(8,128)(2,1)} %get-tuple-element.51), calls=%async_computation.1 | async-start | bytes 393216 | tf_op jit(solution)/shard_map/all_to_all | solution.py:67
Sparse Core Ops, SparseCore 0:
  9.5 66.9 all-gather.1
